TPU v7x, 256 devices: a whole 4x4x8 slice. The times are simulated.
256 devices in a mesh: pb: 4 (over y), neg: 64 (over z, x, core).
Axes of the slice: x: 4, y: 4, z: 8, core: 2. Of those that a mesh axis runs over, the one named last changes fastest.
Arguments:
- hidden: bfloat16 [4, 256, 128, 1024], P('pb', 'neg'), may hold values from -6 to 6
- lengths: int32 [4, 256], P('pb', 'neg'), may hold values from 32 to 128
- teacher: float32 [4, 256], P('pb', 'neg'), may hold values from -8 to 8
- norm_gain: float32 [1024], replicated, may hold values from 0.1 to 1.9
- final_gain: float32 [1024], replicated, may hold values from 0.1 to 1.9
- score_vector: float32 [1024], replicated, may hold values from -0.1875 to 0.1875
- query_weight: bfloat16 [1024, 1024], P(('pb', 'neg')), may hold values from -0.1875 to 0.1875
- key_matrix: bfloat16 [1024, 512], P(('pb', 'neg')), may hold values from -0.1875 to 0.1875
- value_matrix: bfloat16 [1024, 512], P(('pb', 'neg')), may hold values from -0.1875 to 0.1875
- out_weight: bfloat16 [1024, 1024], P(None, ('pb', 'neg')), may hold values from -0.1875 to 0.1875
Outputs:
- scores: float32 [4, 256], P('pb', 'neg')
- loss: float32 [], replicated
- grad_hidden: bfloat16 [4, 256, 128, 1024], P('pb', 'neg')
- grad_query: float32 [1024, 1024], P(('pb', 'neg'))
- grad_key: float32 [1024, 512], P(('pb', 'neg'))
- grad_value: float32 [1024, 512], P(('pb', 'neg'))
- grad_out: float32 [1024, 1024], P(None, ('pb', 'neg'))
Inputs may be any that keep to these rules, and one draw needn't show every extreme that they name: `lengths`: the number of real tokens of the pair; its other positions out of 128 are padding.
All inputs are finite; a program needn't handle non-finite values.
Results may differ from a plain program's by a relative error of at most 0.013.
Values may be sent and summed in bfloat16 or wider, within the bound.
No kernel may reach another device: no remote copies, remote signals or barrier semaphores. Data moves between devices by JAX's collectives and lax.ppermute only.
A program may use at most 64 MiB of HBM per device.

v0:
```python
import jax
import jax.numpy as jnp
from jax import lax
from jax.sharding import Mesh
from jax.sharding import PartitionSpec as P

HEAD_WIDTH = 128
PB_NEG = ("pb", "neg_0", "neg_1", "neg_2")
NEG = ("neg_0", "neg_1", "neg_2")
EPSILON = 1e-06
ROPE_BASE = 1000000.0
TEACHER_TEMP = 2.0
GRAD_SCALE = 512.0


def gather_turned(arrays, axis, dims):
    turned = [jnp.moveaxis(a, dim, 0) for a, dim in zip(arrays, dims)]
    both = jnp.concatenate([t.reshape(len(t), -1) for t in turned], axis=1)
    out, at, outs = (lax.all_gather(both, axis, axis=0, tiled=True), 0, [])
    for t, dim in zip(turned, dims):
        slab = out[:, at : at + t[0].size].reshape(-1, *t.shape[1:])
        outs.append(jnp.moveaxis(slab, 0, dim))
        at += t[0].size
    return tuple(outs)


def from_everyone(shard, axis):
    count = lax.axis_size(axis)
    return lax.all_to_all(
        jnp.broadcast_to(shard[None], (count, *shard.shape)), axis, 0, 0, tiled=True
    )


def taken_together(shard, axis):
    return from_everyone(shard, axis).sum(axis=0)


def in_one(arrays, axis):
    flat, at, outs = (jnp.concatenate([a.reshape(-1) for a in arrays]), 0, [])
    subtotal = taken_together(flat, axis)
    for a in arrays:
        outs.append(subtotal[at : at + a.size].reshape(a.shape))
        at += a.size
    return tuple(outs)


def one_axis_at_a_time(shard, axes):
    for axis in axes:
        shard = lax.psum(shard, axis)
    return shard


def sent_together(arrays, axis, dim, along):
    ends, at = ([], 0)
    for a in arrays[:-1]:
        at += a.shape[along]
        ends.append(at)
    both = jnp.concatenate(arrays, axis=along)
    return tuple(
        jnp.split(lax.psum_scatter(both, axis, scatter_dimension=dim, tiled=True), ends, axis=along)
    )


def cut_along(shard, dim, count):
    before, after = (shard.shape[:dim], shard.shape[dim + 1 :])
    return jnp.moveaxis(shard.reshape(*before, count, -1, *after), dim, 0)


def sum_packed(arrays, axis, dims):
    count = lax.axis_size(axis)
    tiles = [cut_along(a, dim, count) for a, dim in zip(arrays, dims)]
    lines = jnp.concatenate([b.reshape(count, -1) for b in tiles], axis=1)
    span = max(16, -(-lines.shape[1] // 1024) * 8)
    lines = jnp.pad(lines, ((0, 0), (0, span * 128 - lines.shape[1]))).reshape(-1, 128)
    flat, at, outs = (lax.psum_scatter(lines, axis, tiled=True).reshape(-1), 0, [])
    for b in tiles:
        part = b[0]
        outs.append(flat[at : at + part.size].reshape(part.shape))
        at += part.size
    return tuple(outs)


def rope_tables(seq_len, head_size):
    half = head_size // 2
    freqs = ROPE_BASE ** (-(jnp.arange(half, dtype=jnp.float32) * 2.0) / head_size)
    angles = jnp.arange(seq_len, dtype=jnp.float32)[:, None] * freqs[None, :]
    angles = jnp.concatenate([angles, angles], axis=1)
    return (jnp.cos(angles), jnp.sin(angles))


def rotate_half(vector):
    half = vector.shape[-1] // 2
    return jnp.concatenate([-vector[..., half:], vector[..., :half]], axis=-1)


def unrotate_half(vector):
    half = vector.shape[-1] // 2
    return jnp.concatenate([vector[..., half:], -vector[..., :half]], axis=-1)


def forward_pairs(
    tokens_in,
    lengths_here,
    norm_gain,
    final_gain,
    score_vector,
    query_weight,
    key_matrix,
    value_matrix,
    out_weight,
):
    pair_count, seq_len, model_width = tokens_in.shape
    head_count = query_weight.shape[1] // HEAD_WIDTH
    group_count = key_matrix.shape[1] // HEAD_WIDTH
    group_size = head_count // group_count
    inputs_wide = tokens_in.astype(jnp.float32)
    inv_rms = lax.rsqrt(jnp.mean(inputs_wide * inputs_wide, axis=-1, keepdims=True) + EPSILON)
    normed = (inputs_wide * inv_rms * norm_gain).astype(jnp.bfloat16)
    flat_rows = normed.reshape(pair_count * seq_len, model_width)
    key_proj = jnp.dot(flat_rows, key_matrix, preferred_element_type=jnp.float32).reshape(
        pair_count, seq_len, group_count, HEAD_WIDTH
    )
    value_proj = jnp.dot(flat_rows, value_matrix, preferred_element_type=jnp.float32).reshape(
        pair_count, seq_len, group_count, HEAD_WIDTH
    )
    positions = jnp.arange(seq_len, dtype=jnp.int32)
    last_index = lengths_here - 1
    onehot = (positions[None, :] == last_index[:, None]).astype(jnp.float32)
    normed_last = jnp.take_along_axis(normed, last_index[:, None, None], axis=1)[:, 0]
    query_proj = jnp.dot(normed_last, query_weight, preferred_element_type=jnp.float32).reshape(
        pair_count, head_count, HEAD_WIDTH
    )
    query_scale = lax.rsqrt(jnp.mean(query_proj * query_proj, axis=-1, keepdims=True) + EPSILON)
    query_unit = query_proj * query_scale
    key_scale = lax.rsqrt(jnp.mean(key_proj * key_proj, axis=-1, keepdims=True) + EPSILON)
    key_unit = key_proj * key_scale
    cos_table, sin_table = rope_tables(seq_len, HEAD_WIDTH)
    cos_query = jnp.dot(onehot, cos_table, precision=lax.Precision.HIGHEST)
    sin_query = jnp.dot(onehot, sin_table, precision=lax.Precision.HIGHEST)
    query_rot = (
        query_unit * cos_query[:, None, :] + rotate_half(query_unit) * sin_query[:, None, :]
    ).astype(jnp.bfloat16)
    key_rot = (
        key_unit * cos_table[None, :, None, :] + rotate_half(key_unit) * sin_table[None, :, None, :]
    ).astype(jnp.bfloat16)
    value_cast = value_proj.astype(jnp.bfloat16)
    grouped = query_rot.reshape(pair_count, group_count, group_size, HEAD_WIDTH)
    logits = jnp.einsum(
        "pkgd,pskd->pkgs", grouped, key_rot, preferred_element_type=jnp.float32
    ) * HEAD_WIDTH ** (-0.5)
    visible = (positions[None, :] <= last_index[:, None])[:, None, None, :]
    expos = jnp.where(visible, jnp.exp(logits), 0.0)
    attention_weights = expos / jnp.sum(expos, axis=-1, keepdims=True)
    probs_cast = attention_weights.astype(jnp.bfloat16)
    context = jnp.einsum(
        "pkgs,pskd->pkgd", probs_cast, value_cast, preferred_element_type=jnp.float32
    )
    context = context.astype(jnp.bfloat16).reshape(pair_count, head_count * HEAD_WIDTH)
    attended = jnp.dot(context, out_weight, preferred_element_type=jnp.float32)
    residual = jnp.take_along_axis(inputs_wide, last_index[:, None, None], axis=1)[:, 0] + attended
    out_scale = lax.rsqrt(jnp.mean(residual * residual, axis=-1, keepdims=True) + EPSILON)
    out_unit = residual * out_scale
    scores_here = jnp.sum(out_unit * final_gain * score_vector, axis=-1)
    stored = (
        tokens_in,
        onehot,
        inv_rms,
        normed,
        normed_last,
        query_unit,
        query_scale,
        key_unit,
        key_scale,
        cos_query,
        sin_query,
        cos_table,
        sin_table,
        query_rot,
        key_rot,
        value_cast,
        attention_weights,
        probs_cast,
        context,
        out_unit,
        out_scale,
    )
    return (scores_here, stored)


def backward_pairs(
    stored,
    grad_score,
    norm_gain,
    final_gain,
    score_vector,
    query_weight,
    key_matrix,
    value_matrix,
    out_weight,
):
    (
        tokens_in,
        onehot,
        inv_rms,
        normed,
        normed_last,
        query_unit,
        query_scale,
        key_unit,
        key_scale,
        cos_query,
        sin_query,
        cos_table,
        sin_table,
        query_rot,
        key_rot,
        value_cast,
        attention_weights,
        probs_cast,
        context,
        out_unit,
        out_scale,
    ) = stored
    pair_count, seq_len, model_width = tokens_in.shape
    head_count = query_weight.shape[1] // HEAD_WIDTH
    group_count = key_matrix.shape[1] // HEAD_WIDTH
    group_size = head_count // group_count
    grad_unit = grad_score[:, None] * score_vector * final_gain
    grad_resid = out_scale * (
        grad_unit - out_unit * jnp.mean(grad_unit * out_unit, axis=-1, keepdims=True)
    )
    grad_resid_cast = grad_resid.astype(jnp.bfloat16)
    grad_out = jnp.dot(context.T, grad_resid_cast, preferred_element_type=jnp.float32)
    grad_context = jnp.dot(
        grad_resid_cast, out_weight.T, preferred_element_type=jnp.float32
    ).astype(jnp.bfloat16)
    grad_context = grad_context.reshape(pair_count, group_count, group_size, HEAD_WIDTH)
    grad_probs = jnp.einsum(
        "pkgd,pskd->pkgs", grad_context, value_cast, preferred_element_type=jnp.float32
    )
    grad_vals = jnp.einsum(
        "pkgs,pkgd->pskd", probs_cast, grad_context, preferred_element_type=jnp.float32
    )
    spread = jnp.sum(attention_weights * grad_probs, axis=-1, keepdims=True)
    logit_gradient = (attention_weights * (grad_probs - spread)).astype(jnp.bfloat16)
    grouped = query_rot.reshape(pair_count, group_count, group_size, HEAD_WIDTH)
    rotated_query_gradient = jnp.einsum(
        "pkgs,pskd->pkgd", logit_gradient, key_rot, preferred_element_type=jnp.float32
    ) * HEAD_WIDTH ** (-0.5)
    rotated_query_gradient = rotated_query_gradient.reshape(pair_count, head_count, HEAD_WIDTH)
    grad_krot = jnp.einsum(
        "pkgs,pkgd->pskd", logit_gradient, grouped, preferred_element_type=jnp.float32
    ) * HEAD_WIDTH ** (-0.5)
    grad_qunit = rotated_query_gradient * cos_query[:, None, :] + unrotate_half(
        rotated_query_gradient * sin_query[:, None, :]
    )
    grad_kunit = grad_krot * cos_table[None, :, None, :] + unrotate_half(
        grad_krot * sin_table[None, :, None, :]
    )
    grad_qproj = query_scale * (
        grad_qunit - query_unit * jnp.mean(grad_qunit * query_unit, axis=-1, keepdims=True)
    )
    grad_kproj = key_scale * (
        grad_kunit - key_unit * jnp.mean(grad_kunit * key_unit, axis=-1, keepdims=True)
    )
    grad_q_cast = grad_qproj.reshape(pair_count, head_count * HEAD_WIDTH).astype(jnp.bfloat16)
    grad_k_cast = grad_kproj.reshape(pair_count * seq_len, group_count * HEAD_WIDTH).astype(
        jnp.bfloat16
    )
    grad_v_cast = grad_vals.reshape(pair_count * seq_len, group_count * HEAD_WIDTH).astype(
        jnp.bfloat16
    )
    flat_rows = normed.reshape(pair_count * seq_len, model_width)
    grad_query = jnp.dot(normed_last.T, grad_q_cast, preferred_element_type=jnp.float32)
    grad_key = jnp.dot(flat_rows.T, grad_k_cast, preferred_element_type=jnp.float32)
    grad_value = jnp.dot(flat_rows.T, grad_v_cast, preferred_element_type=jnp.float32)
    grad_normed = jnp.dot(grad_k_cast, key_matrix.T, preferred_element_type=jnp.float32)
    grad_normed = grad_normed + jnp.dot(
        grad_v_cast, value_matrix.T, preferred_element_type=jnp.float32
    )
    grad_normed = grad_normed.reshape(pair_count, seq_len, model_width)
    grad_last = jnp.dot(grad_q_cast, query_weight.T, preferred_element_type=jnp.float32)
    grad_normed = grad_normed + onehot[:, :, None] * grad_last[:, None, :]
    inputs_wide = tokens_in.astype(jnp.float32)
    grad_scaled = grad_normed * norm_gain
    grad_input = inv_rms * grad_scaled - inputs_wide * inv_rms * inv_rms * inv_rms * jnp.mean(
        grad_scaled * inputs_wide, axis=-1, keepdims=True
    )
    grad_input = grad_input + onehot[:, :, None] * grad_resid[:, None, :]
    return (grad_input.astype(jnp.bfloat16), (grad_query, grad_key, grad_value, grad_out))


def shards(
    hidden,
    lengths,
    teacher,
    norm_gain,
    final_gain,
    score_vector,
    query_weight,
    key_matrix,
    value_matrix,
    out_weight,
):
    tokens_in = hidden[0]
    lengths_here = lengths[0]
    gathered = gather_turned(
        (query_weight, key_matrix, value_matrix, out_weight), PB_NEG, (0, 0, 0, 1)
    )
    scores_here, stored = forward_pairs(
        tokens_in,
        lengths_here,
        norm_gain,
        final_gain,
        score_vector,
        gathered[0],
        gathered[1],
        gathered[2],
        gathered[3],
    )
    scaled = teacher[0] / TEACHER_TEMP
    expo_s = jnp.exp(scores_here)
    expo_t = jnp.exp(scaled)
    total_s, total_t = in_one((jnp.sum(expo_s), jnp.sum(expo_t)), NEG)
    prob_s = expo_s / total_s
    prob_t = expo_t / total_t
    local_terms = jnp.sum(prob_t * (scaled - jnp.log(total_t) - (scores_here - jnp.log(total_s))))
    loss_value = one_axis_at_a_time(local_terms, PB_NEG)
    grad_score = GRAD_SCALE * (prob_s - prob_t)
    weights_back = gather_turned(
        (query_weight, key_matrix, value_matrix, out_weight), PB_NEG, (0, 0, 0, 1)
    )
    grad_input, grads = backward_pairs(
        stored,
        grad_score,
        norm_gain,
        final_gain,
        score_vector,
        weights_back[0],
        weights_back[1],
        weights_back[2],
        weights_back[3],
    )
    by_query = (
        *tuple(
            (
                part.astype(jnp.float32)
                for part in sent_together(
                    (
                        grads[0].astype(jnp.bfloat16),
                        grads[1].astype(jnp.bfloat16),
                        grads[2].astype(jnp.bfloat16),
                    ),
                    "pb",
                    0,
                    1,
                )
            )
        ),
        lax.psum_scatter(
            grads[3].astype(jnp.bfloat16), "pb", scatter_dimension=1, tiled=True
        ).astype(jnp.float32),
    )
    reduced = sum_packed((by_query[0], by_query[1], by_query[2], by_query[3]), NEG, (0, 0, 0, 1))
    return (
        scores_here[None],
        loss_value,
        grad_input[None],
        reduced[0],
        reduced[1],
        reduced[2],
        reduced[3],
    )


def solution(mesh):
    torus = Mesh(mesh.devices.reshape(mesh.shape["pb"], 8, 4, 2), ("pb", "neg_0", "neg_1", "neg_2"))
    placed = (
        P("pb", NEG, None, None),
        P("pb", NEG),
        P("pb", NEG),
        P(),
        P(),
        P(),
        P(PB_NEG, None),
        P(PB_NEG, None),
        P(PB_NEG, None),
        P(None, PB_NEG),
    )
    return jax.shard_map(
        shards,
        mesh=torus,
        in_specs=placed,
        out_specs=(
            P("pb", NEG),
            P(),
            P("pb", NEG, None, None),
            P(PB_NEG, None),
            P(PB_NEG, None),
            P(PB_NEG, None),
            P(None, PB_NEG),
        ),
        check_vma=False,
    )
```

profile of v0, /device:TPU:8, one launch (start us, length us, event | category | flops | bytes accessed | tf_op | source)
XLA Modules:
  0.0 432.3 jit_solution(12811311809700793395)
XLA Ops:
  7.2 1.4 maximum_bitcast_fusion
  8.7 0.7 compare_select_fusion
  9.4 1.5 multiply_reduce_fusion
  10.9 1.5 multiply_convert_fusion.1
  12.5 0.6 gather_fusion.1
  13.4 0.6 gather_fusion
  14.0 0.6 exponential_reduce_fusion.1
  15.3 0.4 fusion.48
  15.8 1.4 multiply_convert_fusion
  17.2 114.1 %all-gather.3.cloned.1.call-done = bf16[256,4,3072]{2,1,0:T(4,128)(2,1)} async-done(((bf16[1,4,3072]{2,1,0:T(4,128)(2,1)}), bf16[256,4,3072]{2,1,0:T(4,128)(2,1)}) %all-gather.3.cloned.1.call-update) | async-done | bytes 6291472 | tf_op jit(solution)/shard_map/all_gather | solution.py:19
  131.3 10.6 %reshape.509 = bf16[1024,3072]{1,0:T(8,128)(2,1)} reshape(bf16[256,4,3072]{2,1,0:T(4,128)(2,1)} %all-gather.3.cloned.1.call-done) | data formatting | bytes 12582912
  142.0 3.2 fusion.67
  145.2 2.6 copy.98
  147.8 2.5 multiply_reduce_fusion.8
  150.4 1.3 copy.99
  151.8 2.0 multiply_reduce_fusion.2
  153.9 1.1 slice_negate_fusion.1
  154.9 2.3 copy.100
  157.2 3.2 convolution_convert_fusion.5
  161.0 1.4 convolution_convert_fusion.6
  162.4 2.4 multiply_reduce_fusion.7
  164.9 0.6 exponential_reduce_fusion
  165.6 1.4 pad_maximum_fusion.2
  166.9 16.0 %all_to_all.6 = f32[64,1,2]{2,1,0:T(1,128)S(1)} all-to-all(f32[64,1,2]{2,1,0:T(1,128)S(1)} %broadcast_in_dim.39), channel_id=1, replica_groups=mesh['pb'=4,'neg_0'=8,'neg_1'=4,'neg_2'=2] {'neg_0','neg_1','neg_2'}, dimensions={0} | all-to-all | bytes 1024 | tf_op jit(solution)/shard_map/all_to_all | solution.py:29
  183.0 0.6 fusion.73
  183.6 1.3 fusion.55
  185.2 2.0 fusion.13
  187.2 2.1 convolution_convert_fusion
  189.3 0.4 fusion.74
  190.2 0.4 convolution_multiply_fusion
  190.6 0.4 fusion.7
  191.0 1.1 copy.84
  192.1 0.4 broadcast_multiply_fusion
  192.8 1.1 multiply_convert_fusion.2
  194.0 1.5 copy.83
  195.9 0.8 convolution_convert_fusion.1
  196.7 0.8 convolution_convert_fusion.2
  197.4 0.8 convolution_convert_fusion.3
  198.2 2.3 pad_maximum_fusion
  200.6 15.1 %reduce-scatter.6.cloned.1.call-done = bf16[1024,256]{1,0:T(8,128)(2,1)} async-done(((bf16[1024,1024]{1,0:T(8,128)(2,1)}), bf16[1024,256]{1,0:T(8,128)(2,1)}) %reduce-scatter.6.cloned.1.call-update) | async-done | bytes 524304 | tf_op jit(solution)/shard_map/reduce_scatter | solution.py:360
  215.7 1.2 copy.90
  217.2 0.8 copy.91
  218.3 49.3 %reduce-scatter.4.cloned.1.call-done = bf16[256,2048]{0,1:T(8,128)(2,1)} async-done(((bf16[1024,2048]{0,1:T(8,128)(2,1)}), bf16[256,2048]{0,1:T(8,128)(2,1)}) %reduce-scatter.4.cloned.1.call-update) | async-done | bytes 1048592 | tf_op jit(solution)/shard_map/reduce_scatter | solution.py:60
  267.6 1.8 fusion.68
  270.3 1.1 copy.89
  271.6 1.8 maximum_convert_fusion
  273.4 4.3 %reshape.489 = f32[6144,128]{1,0:T(8,128)} reshape(f32[64,12288]{1,0:T(8,128)} %maximum_convert_fusion) | data formatting | bytes 6291456 | tf_op jit(solution)/shard_map/reshape | solution.py:74
  279.1 0.6 fusion.54
  279.8 10.1 %psum.28 = f32[]{:T(128)} all-reduce(f32[]{:T(128)} %fusion.54), channel_id=1, replica_groups=mesh['pb'=4,'neg_0'=8,'neg_1'=4,'neg_2'=2] {'pb'}, use_global_device_ids=true, to_apply=%region_10.11 | all-reduce | flops 1 | bytes 8 | tf_op jit(solution)/shard_map/psum | solution.py:49
  289.9 18.1 %psum.29 = f32[]{:T(128)} all-reduce(f32[]{:T(128)} %psum.28), channel_id=1, replica_groups=mesh['pb'=4,'neg_0'=8,'neg_1'=4,'neg_2'=2] {'neg_0'}, use_global_device_ids=true, to_apply=%region_11.12 | all-reduce | flops 1 | bytes 8 | tf_op jit(solution)/shard_map/psum | solution.py:49
  307.9 11.0 %psum.30 = f32[]{:T(128)} all-reduce(f32[]{:T(128)} %psum.29), channel_id=1, replica_groups=mesh['pb'=4,'neg_0'=8,'neg_1'=4,'neg_2'=2] {'neg_1'}, use_global_device_ids=true, to_apply=%region_12.13 | all-reduce | flops 1 | bytes 8 | tf_op jit(solution)/shard_map/psum | solution.py:49
  319.0 3.1 psum.31
  322.1 2.3 fusion.65
  324.3 2.1 fusion.24
  326.4 2.3 fusion
  328.7 2.5 add_convert_fusion
  331.1 89.9 %reduce-scatter.8.cloned.1.call-done = f32[96,128]{1,0:T(8,128)} async-done(((f32[6144,128]{1,0:T(8,128)}), f32[96,128]{1,0:T(8,128)}) %reduce-scatter.8.cloned.1.call-update) | async-done | bytes 49168 | tf_op jit(solution)/shard_map/reduce_scatter | solution.py:75
  421.1 0.7 fusion.71
  421.8 0.6 reshape.483
  422.4 0.6 reshape.482
  423.0 0.7 fusion.70
  423.8 0.6 reshape.481
  424.4 0.5 reshape.484
  424.9 0.8 copy.93
  (91 shorter events, 5.6 us)
Async XLA Ops:
  7.2 6.0 %copy-start = (bf16[1,4,128,1024]{3,2,1,0:T(8,128)(2,1)S(1)}, bf16[1,4,128,1024]{3,2,1,0:T(8,128)(2,1)}, u32[]{:S(2)}) copy-start(bf16[1,4,128,1024]{3,2,1,0:T(8,128)(2,1)} %param.10) | copy-start | bytes 3145732
  7.2 124.1 %all-gather.3.cloned.1.call-start = ((), (), s32[]{:S(2)}) async-start(), calls=%async_computation.7 | async-start | bytes 6316032 | tf_op jit(solution)/shard_map/all_gather | solution.py:19
  8.7 207.0 %reduce-scatter.6.cloned.1.call-start = ((), (), s32[]{:S(2)}) async-start(), calls=%async_computation.5 | async-start | bytes 2621440 | tf_op jit(solution)/shard_map/reduce_scatter | solution.py:360
  12.5 1.5 copy-start.13
  12.5 2.4 copy-start.14
  12.5 3.3 copy-start.9
  142.0 3.3 slice-start
  147.8 2.6 copy-start.1
  147.8 4.0 copy-start.6
  157.2 3.3 copy-start.2
  157.2 3.3 copy-start.3
  160.7 4.0 copy-start.10
  160.7 4.0 copy-start.11
  164.9 114.2 %copy-start.12 = (f32[4]{0:T(128)}, f32[4]{0:T(128)S(1)}, u32[]{:S(2)}) copy-start(f32[4]{0:T(128)S(1)} %multiply_reduce_fusion.6) | copy-start | bytes 52
  185.2 4.1 copy-start.8
  189.9 77.7 %reduce-scatter.4.cloned.1.call-start = ((), (), s32[]{:S(2)}) async-start(), calls=%async_computation.4 | async-start | bytes 5242880 | tf_op jit(solution)/shard_map/reduce_scatter | solution.py:60
  194.0 2.7 copy-start.4
  194.0 2.7 copy-start.7
  200.6 220.5 %reduce-scatter.8.cloned.1.call-start = ((), (), s32[]{:S(2)}) async-start(), calls=%async_computation.6 | async-start | bytes 3194880 | tf_op jit(solution)/shard_map/reduce_scatter | solution.py:75
  267.6 2.1 slice-start.1
  324.3 2.1 copy-start.5
Sparse Core Ops, SparseCore 0:
  12.4 118.8 all-gather.2
  190.0 25.6 reduce-scatter.5
  218.4 49.1 reduce-scatter.3
  277.9 143.1 reduce-scatter.7
where the time goes:
time: 433 us; the launch traced here: 432 us
  waiting for transfers between devices  269 us (62%)
  blocking collectives  58.3 us (13%)
  local copies, waits for them, and re-layouts  39.9 us (9%)
  matrix products  26.8 us (6%)
  other arithmetic  22.8 us (5%)
  between operations  15.6 us (4%)
    all_gather x1, waiting for transfers between devices, gather_turned(): out, at, outs = (lax.all_gather(both, axis, axis=0, tiled=True), 0, [])  114 us
    reduce_scatter x1, waiting for transfers between devices, sum_packed(): lax.psum_scatter(lines, axis, tiled=True).reshape(-1)  89.9 us
    reduce_scatter x1, waiting for transfers between devices, sent_together(): lax.psum_scatter(both, axis, scatter_dimension=dim, tiled=True)  49.3 us
    psum x4, blocking collectives, one_axis_at_a_time(): shard = lax.psum(shard, axis)  42.3 us
    unnamed x39, local copies, waits for them, and re-layouts  20.9 us
    all_to_all x1, blocking collectives, from_everyone(): lax.all_to_all(jnp.broadcast_to(shard[None], (count, *shard.shape)), axis...  16 us
    reduce_scatter x1, waiting for transfers between devices, shards(): lax.psum_scatter(grads[3].astype(jnp.bfloat16), 'pb', scatter_dimension=1...  15.1 us
  transfers between devices with their start and end apart: 4, of which 4 were waited for; matrix products, arithmetic and copies ran while one was open for 7% of the time, Pallas kernels for 0%

commit v1 on v0

--- a/solution.py
+++ b/solution.py
@@ -16,7 +16,13 @@
 def gather_turned(arrays, axis, dims):
     turned = [jnp.moveaxis(a, dim, 0) for a, dim in zip(arrays, dims)]
     both = jnp.concatenate([t.reshape(len(t), -1) for t in turned], axis=1)
-    out, at, outs = (lax.all_gather(both, axis, axis=0, tiled=True), 0, [])
+    out, at, outs = (
+        jnp.concatenate(
+            lax.all_to_all(jnp.stack([both] * lax.axis_size(axis)), axis, 0, 0), axis=0
+        ),
+        0,
+        [],
+    )
     for t, dim in zip(turned, dims):
         slab = out[:, at : at + t[0].size].reshape(-1, *t.shape[1:])
         outs.append(jnp.moveaxis(slab, 0, dim))

time: 433 us -> 470 us (1.085)
  waiting for transfers between devices: 269 us -> 291 us
  starting transfers between devices: 0.34 us -> 15.6 us
    all_to_all x0 -> x1, waiting for transfers between devices: none -> 135 us  [gather_turned(): lax.all_to_all(jnp.stack([both] * lax.axis_size(axis)), axis, 0, 0)]
    all_gather x1 -> x0, waiting for transfers between devices: 114 us -> none  [gather_turned(): out, at, outs = (lax.all_gather(both, axis, axis=0, tiled=True), 0, [])]
    unnamed x39 -> x30, local copies, waits for them, and re-layouts: 20.9 us -> 1.07 us
    all_to_all x0 -> x1, starting transfers between devices: none -> 15.5 us  [gather_turned(): lax.all_to_all(jnp.stack([both] * lax.axis_size(axis)), axis, 0, 0)]
    dot_general x0 -> x5, local copies, waits for them, and re-layouts: none -> 11.4 us  [the longest x2 7.04 us: forward_pairs(): jnp.dot(normed_last, query_weight, preferred_element_type=jnp.float32)]
    reshape x0 -> x1, local copies, waits for them, and re-layouts: none -> 10.6 us  [gather_turned(): jnp.concatenate(lax.all_to_all(jnp.stack([both] * lax.axis_size(axis)), a...]
  transfers between devices with their start and end apart: 4 -> 4, of which waited for: 4 -> 4; matrix products, arithmetic and copies ran while one was open for 7% -> 5% of each run, Pallas kernels for 0% -> 0%
where the time goes in v1:
time: 470 us; the launch traced here: 469 us
  waiting for transfers between devices  291 us (62%)
  blocking collectives  58.8 us (13%)
  local copies, waits for them, and re-layouts  43.6 us (9%)
  matrix products  25.1 us (5%)
  other arithmetic  19 us (4%)
  starting transfers between devices  15.6 us (3%)
  between operations  15.6 us (3%)
    all_to_all x1, waiting for transfers between devices, gather_turned(): lax.all_to_all(jnp.stack([both] * lax.axis_size(axis)), axis, 0, 0)  135 us
    reduce_scatter x1, waiting for transfers between devices, sum_packed(): lax.psum_scatter(lines, axis, tiled=True).reshape(-1)  89.8 us
    reduce_scatter x1, waiting for transfers between devices, sent_together(): lax.psum_scatter(both, axis, scatter_dimension=dim, tiled=True)  49.2 us
    psum x4, blocking collectives, one_axis_at_a_time(): shard = lax.psum(shard, axis)  42.5 us
    reduce_scatter x1, waiting for transfers between devices, shards(): lax.psum_scatter(grads[3].astype(jnp.bfloat16), 'pb', scatter_dimension=1...  16.6 us
    all_to_all x1, blocking collectives, from_everyone(): lax.all_to_all(jnp.broadcast_to(shard[None], (count, *shard.shape)), axis...  16.2 us
    all_to_all x1, starting transfers between devices, gather_turned(): lax.all_to_all(jnp.stack([both] * lax.axis_size(axis)), axis, 0, 0)  15.5 us
    reshape x1, local copies, waits for them, and re-layouts, gather_turned(): jnp.concatenate(lax.all_to_all(jnp.stack([both] * lax.axis_size(axis)), a...  10.6 us
  transfers between devices with their start and end apart: 4, of which 4 were waited for; matrix products, arithmetic and copies ran while one was open for 5% of the time, Pallas kernels for 0%

profile of v1, /device:TPU:8, one launch (start us, length us, event | category | flops | bytes accessed | tf_op | source)
XLA Modules:
  0.0 468.7 jit_solution(1111580443258722624)
XLA Ops:
  7.2 0.8 pad_maximum_fusion.2
  7.9 4.3 stack.2
  12.2 15.5 %all-to-all-start = ((bf16[256,4,3072]{2,1,0:T(4,128)(2,1)}), bf16[256,4,3072]{2,1,0:T(4,128)(2,1)}, u32[]{:S(2)}, u32[]{:S(2)}) async-start(bf16[256,4,3072]{2,1,0:T(4,128)(2,1)} %stack.2), calls=%async_computation | async-start | bytes 12582912 | tf_op jit(solution)/shard_map/all_to_all | solution.py:21
  28.5 0.6 gather_fusion.1
  29.3 0.6 gather_fusion
  29.9 0.6 exponential_reduce_fusion.1
  30.9 0.3 fusion.51
  31.2 0.4 fusion.52
  31.7 1.4 multiply_convert_fusion
  33.1 135.2 %all-to-all-done = bf16[256,4,3072]{2,1,0:T(4,128)(2,1)} async-done(((bf16[256,4,3072]{2,1,0:T(4,128)(2,1)}), bf16[256,4,3072]{2,1,0:T(4,128)(2,1)}, u32[]{:S(2)}, u32[]{:S(2)}) %all-to-all-start) | async-done | bytes 6291488 | tf_op jit(solution)/shard_map/all_to_all | solution.py:21
  168.3 10.6 %reshape.474 = bf16[1024,3072]{1,0:T(8,128)(2,1)} reshape(bf16[256,4,3072]{2,1,0:T(4,128)(2,1)} %all-to-all-done) | data formatting | bytes 12582912 | tf_op jit(solution)/shard_map/reshape | solution.py:20
  179.0 1.7 slice_bitcast_fusion.2
  180.7 3.1 slice_bitcast_fusion
  183.8 1.3 copy.61
  185.1 1.4 copy.58
  186.5 2.8 convolution_convert_fusion.5
  189.3 0.8 multiply_reduce_fusion.2
  190.2 0.9 slice_negate_fusion.1
  191.1 3.9 copy.57
  195.0 2.4 multiply_reduce_fusion.8
  198.2 1.4 convolution_convert_fusion.6
  199.5 2.4 multiply_reduce_fusion.7
  202.1 0.6 exponential_reduce_fusion
  202.7 1.4 pad_maximum_fusion.3
  204.1 16.2 %all_to_all.12 = f32[64,1,2]{2,1,0:T(1,128)S(1)} all-to-all(f32[64,1,2]{2,1,0:T(1,128)S(1)} %broadcast_in_dim.39), channel_id=1, replica_groups=mesh['pb'=4,'neg_0'=8,'neg_1'=4,'neg_2'=2] {'neg_0','neg_1','neg_2'}, dimensions={0} | all-to-all | bytes 1024 | tf_op jit(solution)/shard_map/all_to_all | solution.py:35
  220.4 0.6 fusion.72
  221.0 1.3 fusion.59
  222.6 2.0 fusion.15
  224.7 2.1 convolution_convert_fusion
  226.7 0.4 fusion.73
  227.5 0.4 convolution_multiply_fusion
  227.8 0.4 broadcast_multiply_fusion
  228.6 0.4 multiply_convert_fusion.2
  229.3 0.4 fusion.9
  230.5 0.8 convolution_convert_fusion.1
  231.5 0.8 convolution_convert_fusion.2
  232.3 0.8 convolution_convert_fusion.3
  233.0 2.3 pad_maximum_fusion
  235.4 16.6 %reduce-scatter.6.cloned.1.call-done = bf16[1024,256]{1,0:T(8,128)(2,1)} async-done(((bf16[1024,1024]{1,0:T(8,128)(2,1)}), bf16[1024,256]{1,0:T(8,128)(2,1)}) %reduce-scatter.6.cloned.1.call-update) | async-done | bytes 524304 | tf_op jit(solution)/shard_map/reduce_scatter | solution.py:366
  252.0 1.2 copy.71
  253.5 0.8 copy.72
  254.3 0.3 copy.73
  254.7 49.2 %reduce-scatter.4.cloned.1.call-done = bf16[256,2048]{0,1:T(8,128)(2,1)} async-done(((bf16[1024,2048]{0,1:T(8,128)(2,1)}), bf16[256,2048]{0,1:T(8,128)(2,1)}) %reduce-scatter.4.cloned.1.call-update) | async-done | bytes 1048592 | tf_op jit(solution)/shard_map/reduce_scatter | solution.py:66
  303.9 1.1 fusion.67
  305.5 0.9 reshape_reshape.13
  306.9 2.8 maximum_convert_fusion
  309.7 4.3 reshape.496
  315.4 0.6 fusion.58
  316.0 10.1 %psum.28 = f32[]{:T(128)} all-reduce(f32[]{:T(128)} %fusion.58), channel_id=1, replica_groups=mesh['pb'=4,'neg_0'=8,'neg_1'=4,'neg_2'=2] {'pb'}, use_global_device_ids=true, to_apply=%region_10.11 | all-reduce | flops 1 | bytes 8 | tf_op jit(solution)/shard_map/psum | solution.py:55
  326.2 18.1 %psum.29 = f32[]{:T(128)} all-reduce(f32[]{:T(128)} %psum.28), channel_id=1, replica_groups=mesh['pb'=4,'neg_0'=8,'neg_1'=4,'neg_2'=2] {'neg_0'}, use_global_device_ids=true, to_apply=%region_11.12 | all-reduce | flops 1 | bytes 8 | tf_op jit(solution)/shard_map/psum | solution.py:55
  344.3 11.0 %psum.30 = f32[]{:T(128)} all-reduce(f32[]{:T(128)} %psum.29), channel_id=1, replica_groups=mesh['pb'=4,'neg_0'=8,'neg_1'=4,'neg_2'=2] {'neg_1'}, use_global_device_ids=true, to_apply=%region_12.13 | all-reduce | flops 1 | bytes 8 | tf_op jit(solution)/shard_map/psum | solution.py:55
  355.3 3.3 psum.31
  358.6 2.3 fusion.7
  360.8 2.1 fusion.24
  362.9 2.3 fusion
  365.2 2.5 add_convert_fusion
  367.7 89.8 %reduce-scatter.8.cloned.1.call-done = f32[96,128]{1,0:T(8,128)} async-done(((f32[6144,128]{1,0:T(8,128)}), f32[96,128]{1,0:T(8,128)}) %reduce-scatter.8.cloned.1.call-update) | async-done | bytes 49168 | tf_op jit(solution)/shard_map/reduce_scatter | solution.py:81
  457.5 0.7 fusion.69
  458.3 0.6 reshape.488
  458.9 0.7 fusion.70
  459.6 0.6 reshape.489
  460.2 0.6 reshape.490
  460.8 0.5 reshape.491
  461.3 0.8 copy.74
  (88 shorter events, 6.0 us)
Async XLA Ops:
  12.2 15.5 %copy-start.13 = (s32[1,4]{1,0:T(1,128)S(1)}, s32[1,4]{1,0:T(1,128)}, u32[]{:S(2)}) copy-start(s32[1,4]{1,0:T(1,128)} %param.11) | copy-start | bytes 52
  12.2 15.6 %copy-start = (bf16[1,4,128,1024]{3,2,1,0:T(8,128)(2,1)S(1)}, bf16[1,4,128,1024]{3,2,1,0:T(8,128)(2,1)}, u32[]{:S(2)}) copy-start(bf16[1,4,128,1024]{3,2,1,0:T(8,128)(2,1)} %param.10) | copy-start | bytes 3145732
  12.2 15.9 %copy-start.8 = (f32[1024]{0:T(1024)S(1)}, f32[1024]{0:T(1024)}, u32[]{:S(2)}) copy-start(f32[1024]{0:T(1024)} %param.13) | copy-start | bytes 12292
  12.2 156.1 %all-to-all-start = ((bf16[256,4,3072]{2,1,0:T(4,128)(2,1)}), bf16[256,4,3072]{2,1,0:T(4,128)(2,1)}, u32[]{:S(2)}, u32[]{:S(2)}) async-start(bf16[256,4,3072]{2,1,0:T(4,128)(2,1)} %stack.2), calls=%async_computation | async-start | bytes 12582912 | tf_op jit(solution)/shard_map/all_to_all | solution.py:21
  27.7 224.3 %reduce-scatter.6.cloned.1.call-start = ((), (), s32[]{:S(2)}) async-start(), calls=%async_computation.6 | async-start | bytes 2621440 | tf_op jit(solution)/shard_map/reduce_scatter | solution.py:366
  28.4 1.5 copy-start.12
  185.1 1.4 copy-start.4
  186.5 2.8 copy-start.6
  195.0 2.6 copy-start.1
  197.8 4.1 copy-start.9
  197.8 4.1 copy-start.10
  202.1 113.3 %copy-start.11 = (f32[4]{0:T(128)}, f32[4]{0:T(128)S(1)}, u32[]{:S(2)}) copy-start(f32[4]{0:T(128)S(1)} %multiply_reduce_fusion.6) | copy-start | bytes 52
  222.6 4.1 copy-start.7
  227.3 76.6 %reduce-scatter.4.cloned.1.call-start = ((), (), s32[]{:S(2)}) async-start(), calls=%async_computation.5 | async-start | bytes 5242880 | tf_op jit(solution)/shard_map/reduce_scatter | solution.py:66
  230.1 2.2 copy-start.2
  230.1 1.4 copy-start.5
  235.4 222.1 %reduce-scatter.8.cloned.1.call-start = ((), (), s32[]{:S(2)}) async-start(), calls=%async_computation.7 | async-start | bytes 3194880 | tf_op jit(solution)/shard_map/reduce_scatter | solution.py:81
  303.9 2.5 slice-start
  360.8 2.1 copy-start.3
Sparse Core Ops, SparseCore 0:
  227.4 24.5 reduce-scatter.5
  254.8 49.1 reduce-scatter.3
  314.2 143.3 reduce-scatter.7
